TPU v7x, 128 devices: a whole 4x4x4 slice. The times are simulated.
128 devices in a mesh: dp: 8 (over x, y_hi), seq: 16 (over y_lo, z, core).
Axes of the slice: x: 4, y: 4 (y_hi: 2, y_lo: 2; y = y_hi * 2 + y_lo), z: 4, core: 2. Of those that a mesh axis runs over, the one named last changes fastest.
Arguments:
- caption_states: bfloat16 [8, 128, 4096], P('dp', None, 'seq'), may hold values from -1600 to 1600
- caption_gain: float32 [4096], P('seq'), may hold values from 0.25 to 2.5
- text_proj: bfloat16 [4096, 4608], P('seq'), may hold values from -0.09375 to 0.09375
- caption_len: int32 [8], P('dp'), may hold values from 1 to 128, 640 in all
- slot_source: int32 [8, 128], P('dp'), may hold values from 0 to 127, each once within a row
- query_gain: float32 [128], replicated, may hold values from 0.5 to 2
- key_gain: float32 [128], replicated, may hold values from 0.5 to 2
- image_q: bfloat16 [8, 2048, 1536], P('dp', 'seq'), may hold values from -34 to 34
- image_k: bfloat16 [8, 2048, 1536], P('dp', 'seq'), may hold values from -6.5 to 6.5
- image_v: bfloat16 [8, 2048, 1536], P('dp', 'seq'), may hold values from -6 to 6
- out_weight: bfloat16 [3072, 1536], replicated, may hold values from -0.15625 to 0.15625
- gate: float32 [8, 3072], P('dp'), may hold values from -4 to 4
- d_out: bfloat16 [8, 2048, 3072], P('dp', 'seq'), may hold values from -2.5 to 2.5
Outputs:
- image_out: bfloat16 [8, 2048, 3072], P('dp', 'seq')
- text_attn: bfloat16 [8, 128, 1536], P('dp', 'seq')
- d_attn: bfloat16 [8, 2048, 1536], P('dp', 'seq')
- grad_wo: float32 [3072, 1536], P(('dp', 'seq'))
- grad_gate: float32 [8, 3072], P('dp', 'seq')
Inputs may be any that keep to these rules, and one draw needn't show every extreme that they name: `caption_len`: caption lengths in tokens; the longest is 128. `slot_source`: each row is a permutation: every caption row of the sequence sits in exactly one slot; slots whose row is not below the caption's length are padding.
All inputs are finite; a program needn't handle non-finite values. No bound on the sum of `caption_len` on one device may be relied on, other than what follows from the above.
Results may differ from a plain program's by a relative error of at most 0.0095.
Values may be sent and summed in bfloat16 or wider, within the bound.
A program may use at most 128 MiB of HBM per device.

v0:
```python
import jax
import jax.numpy as jnp
from jax import lax
from jax.sharding import PartitionSpec as P

DT5 = 4096


neg_big = -1e30
eps_norm = 1e-06


def head_norm(values_in, gain_vec):
    shaped = values_in.reshape(values_in.shape[0], -1, gain_vec.shape[0])
    normed = (
        shaped * lax.rsqrt(jnp.mean(shaped * shaped, axis=-1, keepdims=True) + eps_norm) * gain_vec
    )
    return normed.reshape(values_in.shape).astype(jnp.bfloat16)


def text_heads(summed, squares, query_gain, key_gain, inner_width):
    factor = lax.rsqrt(squares / DT5 + eps_norm)
    normed = summed * factor[:, None]
    text_query = head_norm(normed[:, :inner_width], query_gain)
    text_key = head_norm(normed[:, inner_width : 2 * inner_width], key_gain)
    text_value = normed[:, 2 * inner_width :].astype(jnp.bfloat16)
    return (text_query, text_key, text_value)


def start_state(query_heads):
    query_count, head_count, head_size = query_heads.shape
    return (
        jnp.full((head_count, query_count), neg_big, jnp.float32),
        jnp.zeros((head_count, query_count), jnp.float32),
        jnp.zeros((head_count, query_count, head_size), jnp.float32),
    )


def attend(running, query_heads, key_rows, value_rows, usable):
    max_old, total_old, weighted = running
    count_keys = key_rows.shape[0]
    head_size = query_heads.shape[2]
    key_heads = key_rows.reshape(count_keys, -1, head_size)
    value_heads = value_rows.reshape(count_keys, -1, head_size)
    scores = jnp.einsum(
        "qhd,khd->hqk", query_heads, key_heads, preferred_element_type=jnp.float32
    ) * head_size ** (-0.5)
    scores = jnp.where(usable[None, None, :], scores, neg_big)
    max_new = jnp.maximum(max_old, jnp.max(scores, axis=-1))
    weights_now = jnp.where(usable[None, None, :], jnp.exp(scores - max_new[..., None]), 0.0)
    total_new = jnp.sum(weights_now, axis=-1)
    weighted = jnp.einsum(
        "hqk,khd->hqd",
        weights_now.astype(jnp.bfloat16),
        value_heads,
        preferred_element_type=jnp.float32,
    )
    return (max_new, total_new, weighted)


def on_device(
    caption_states,
    caption_gain,
    text_proj,
    caption_len,
    slot_source,
    query_gain,
    key_gain,
    image_q,
    image_k,
    image_v,
    out_weight,
    gate,
    d_out,
):
    seq_count = lax.axis_size("seq")
    seq_index = lax.axis_index("seq")
    slot_total = slot_source.shape[1]
    slot_local = slot_total // seq_count
    image_local = image_q.shape[1]
    inner_width = image_q.shape[2]
    head_size = query_gain.shape[0]
    sources = slot_source[0]
    picked = jnp.take(caption_states[0], sources, axis=0).astype(jnp.float32)
    scaled_rows = (picked * caption_gain).astype(jnp.bfloat16)
    partial_proj = jnp.dot(scaled_rows, text_proj, preferred_element_type=jnp.float32)
    partial_squares = jnp.sum(picked * picked, axis=1)
    usable_slots = sources < caption_len[0]
    own_usable = lax.dynamic_slice_in_dim(usable_slots, seq_index * slot_local, slot_local)
    summed, squares = (
        lax.psum_scatter(partial_proj, "seq", scatter_dimension=0, tiled=True),
        lax.psum_scatter(partial_squares, "seq", scatter_dimension=0, tiled=True),
    )
    text_query, text_key, text_value = text_heads(
        summed, squares, query_gain, key_gain, inner_width
    )
    queries = jnp.concatenate([image_q[0], text_query], axis=0)
    query_heads = queries.reshape(queries.shape[0], -1, head_size)
    key_rows = jnp.concatenate([image_k[0], text_key], axis=0)
    value_rows = jnp.concatenate([image_v[0], text_value], axis=0)
    usable_all = jnp.concatenate(
        [
            jnp.ones((seq_count, image_local), dtype=jnp.bool_),
            usable_slots.reshape(seq_count, slot_local),
        ],
        axis=1,
    ).reshape(-1)
    running = attend(
        start_state(query_heads),
        query_heads,
        lax.all_gather(key_rows, "seq", axis=0, tiled=True),
        lax.all_gather(value_rows, "seq", axis=0, tiled=True),
        usable_all,
    )
    max_final, total_final, weighted = running
    attention = (
        jnp.transpose(weighted / total_final[..., None], (1, 0, 2))
        .reshape(-1, inner_width)
        .astype(jnp.bfloat16)
    )
    image_attn = attention[:image_local]
    text_attn = jnp.where(own_usable[:, None], attention[image_local:], jnp.zeros((), jnp.bfloat16))
    projected = lax.dot_general(
        image_attn, out_weight, (((1,), (1,)), ((), ())), preferred_element_type=jnp.float32
    )
    gate_row = gate[0]
    image_out = (gate_row * projected).astype(jnp.bfloat16)
    cotangent = d_out[0].astype(jnp.float32)
    gated_grad = (gate_row * cotangent).astype(jnp.bfloat16)
    gate_term = jnp.sum(projected * cotangent, axis=0)
    d_attn = jnp.dot(gated_grad, out_weight, preferred_element_type=jnp.float32).astype(
        jnp.bfloat16
    )
    grad_wo = lax.psum_scatter(
        lax.dot_general(
            gated_grad, image_attn, (((0,), (0,)), ((), ())), preferred_element_type=jnp.float32
        ),
        ("dp", "seq"),
        scatter_dimension=0,
        tiled=True,
    )
    grad_gate = lax.psum_scatter(gate_term, "seq", scatter_dimension=0, tiled=True)
    return (image_out[None], text_attn[None], d_attn[None], grad_wo, grad_gate[None])


def solution(mesh):
    in_specs = (
        P("dp", None, "seq"),
        P("seq"),
        P("seq", None),
        P("dp"),
        P("dp", None),
        P(),
        P(),
        P("dp", "seq", None),
        P("dp", "seq", None),
        P("dp", "seq", None),
        P(),
        P("dp", None),
        P("dp", "seq", None),
    )
    out_specs = (
        P("dp", "seq", None),
        P("dp", "seq", None),
        P("dp", "seq", None),
        P(("dp", "seq"), None),
        P("dp", "seq"),
    )
    return jax.shard_map(
        on_device, mesh=mesh, in_specs=in_specs, out_specs=out_specs, check_vma=False
    )
```

profile of v0, /device:TPU:1, one launch (start us, length us, event | category | flops | bytes accessed | tf_op | source)
XLA Modules:
  0.0 445.1 jit_solution(14536937245673772686)
XLA Ops:
  7.2 0.0 copy-start
  7.2 0.0 copy-start.9
  7.2 0.0 copy-start.7
  7.2 0.0 copy-start.8
  7.2 0.0 reduce-scatter.3.cloned.1.call-start
  8.1 0.7 fusion.38
  8.8 0.7 bitcast_compare_fusion
  9.5 1.6 gather_fusion
  11.1 0.0 copy-done
  11.1 2.6 fusion.28
  13.7 0.0 reduce-scatter.3.cloned.1.call-update
  13.7 0.0 all-gather.3.cloned.1.call-start
  13.8 1.2 dynamic-slice
  15.7 0.2 fusion.27
  15.9 29.4 %all-reduce.1 = f32[128]{0:T(128)S(1)} all-reduce(f32[128]{0:T(128)S(1)} %fusion.27), channel_id=3, replica_groups=mesh['dp'=8,'seq'=16] {'seq'}, use_global_device_ids=true, to_apply=%region_2.3.clone | all-reduce | flops 128 | bytes 1024
  45.2 0.1 fusion.40
  45.3 0.7 broadcast_bitcast_fusion
  46.0 31.3 %reduce-scatter.3.cloned.1.call-done = f32[8,4608]{1,0:T(8,128)} async-done(((f32[128,4608]{1,0:T(8,128)}), f32[8,4608]{1,0:T(8,128)}) %reduce-scatter.3.cloned.1.call-update) | async-done | bytes 147472 | tf_op jit(solution)/shard_map/reduce_scatter | solution.py:91
  77.3 1.0 broadcast_multiply_fusion
  78.3 0.1 bitcast_reduce_fusion.1
  78.4 0.1 fusion.35
  78.5 1.8 pad_maximum_fusion
  80.3 0.0 all-gather.3.cloned.1.call-update
  80.3 0.0 all-gather.5.cloned.1.call-start
  80.4 0.0 copy-done.7
  80.4 0.8 pad_maximum_fusion.1
  81.2 0.0 all-gather.5.cloned.1.call-update
  81.2 0.0 reduce-scatter.5.cloned.1.call-start
  81.3 0.0 copy-done.9
  81.3 0.1 lt.40
  81.4 0.1 broadcast_in_dim.67
  81.5 0.0 copy-done.8
  81.5 0.2 copy.27
  81.8 0.2 copy.28
  82.0 45.1 %all-gather.3.cloned.1.call-done = bf16[2176,1536]{1,0:T(8,128)(2,1)} async-done(((bf16[136,1536]{1,0:T(8,128)(2,1)}), bf16[2176,1536]{1,0:T(8,128)(2,1)}) %all-gather.3.cloned.1.call-update) | async-done | bytes 6684688 | tf_op jit(solution)/shard_map/all_gather | solution.py:111
  127.1 9.3 %copy.29 = bf16[2176,1536]{0,1:T(8,128)(2,1)} copy(bf16[2176,1536]{1,0:T(8,128)(2,1)} %all-gather.3.cloned.1.call-done) | data formatting | bytes 13369344 | tf_op jit(solution)/shard_map/all_gather | solution.py:111
  136.4 4.8 %fusion = (f32[12,136]{1,0:T(8,128)S(1)}, f32[12,136,2176]{2,1,0:T(8,128)S(1)}) fusion(pred[2176]{0:T(1024)(128)(4,1)S(1)} %broadcast_in_dim.67, bf16[2176,12,128]{0,2,1:T(8,128)(2,1)} %bitcast.78, bf16[8,12,128]{2,0,1:T(8,128)(2,1)S(1)} %get-tuple-element.9, bf16[128,12,128]{2,0,1:T(8,128)(2,1)S(1)} %copy.28), kind=kOutput, calls=%fused_computation.3 | convolution fusion | flops 920603008 | bytes 21316096 | tf_op jit(solution)/shard_map/qhd,khd->hqk/dot_general | solution.py:45
  141.2 0.0 copy-start.2
  141.2 5.1 %copy-done.2 = f32[12,136,2176]{2,1,0:T(8,128)} copy-done((f32[12,136,2176]{2,1,0:T(8,128)}, f32[12,136,2176]{2,1,0:T(8,128)S(1)}, u32[]{:S(2)}) %copy-start.2) | copy-done | bytes 14204952
  146.3 3.8 fusion.1
  150.1 24.5 %all-gather.5.cloned.1.call-done = bf16[2176,1536]{1,0:T(8,128)(2,1)} async-done(((bf16[136,1536]{1,0:T(8,128)(2,1)}), bf16[2176,1536]{1,0:T(8,128)(2,1)}) %all-gather.5.cloned.1.call-update) | async-done | bytes 6684688 | tf_op jit(solution)/shard_map/all_gather | solution.py:112
  174.5 9.4 %copy.31 = bf16[2176,1536]{0,1:T(8,128)(2,1)} copy(bf16[2176,1536]{1,0:T(8,128)(2,1)} %all-gather.5.cloned.1.call-done) | data formatting | bytes 13369344 | tf_op jit(solution)/shard_map/all_gather | solution.py:112
  183.9 10.4 %fusion.15 = bf16[136,12,128]{2,0,1:T(8,128)(2,1)S(1)} fusion(bf16[2176,12,128]{0,2,1:T(8,128)(2,1)} %bitcast.79, f32[12,136,2176]{2,1,0:T(8,128)} %copy-done.2, f32[12,136]{1,0:T(8,128)S(1)} %broadcast_maximum_fusion, pred[2176]{0:T(1024)(128)(4,1)S(1)} %broadcast_in_dim.67, f32[136,12]{0,1:T(8,128)S(1)} %bitcast.89), kind=kOutput, calls=%fused_computation.17 | convolution fusion | flops 927289344 | bytes 21322624 | tf_op jit(solution)/shard_map/hqk,khd->hqd/dot_general | solution.py:52
  194.3 0.0 copy-start.5
  194.4 0.2 copy.33
  194.6 0.0 copy-start.4
  194.6 0.0 copy-done.3
  194.6 0.0 copy-done.6
  194.6 8.0 %fusion.19 = f32[3072,1536]{1,0:T(8,128)} fusion(bf16[128,1536]{0,1:T(8,128)(2,1)S(1)} %bitcast.81, bf16[1,128,3072]{2,1,0:T(8,128)(2,1)S(1)} %copy-done.3, f32[3072]{0:T(1024)S(1)} %bitcast.84), kind=kOutput, calls=%fused_computation.19 | convolution fusion | flops 1209139200 | bytes 20066304 | tf_op jit(solution)/shard_map/dot_general | solution.py:135
  202.7 0.0 copy-done.5
  202.7 0.0 copy-done.4
  202.7 0.0 reduce-scatter.5.cloned.1.call-update
  202.7 0.0 slice-start
  203.5 0.1 dynamic_slice.3
  203.5 6.2 %fusion.6 = bf16[1,128,1536]{2,1,0:T(8,128)(2,1)} fusion(bf16[3072,1536]{1,0:T(8,128)(2,1)} %param.23, bf16[1,128,3072]{2,1,0:T(8,128)(2,1)} %param.25, f32[3072]{0:T(1024)S(1)} %bitcast.85), kind=kOutput, calls=%fused_computation.9 | convolution fusion | flops 1209335808 | bytes 10629120 | tf_op jit(solution)/shard_map/dot_general | solution.py:131
  209.8 0.0 slice-done
  209.8 0.0 slice-done.1
  209.8 0.2 slice-done.2
  210.0 5.4 %fusion.8 = (f32[3072]{0:T(1024)S(1)}, bf16[1,128,3072]{2,1,0:T(8,128)(2,1)}) fusion(bf16[1,128,3072]{2,1,0:T(8,128)(2,1)} %param.25, f32[3072]{0:T(1024)S(1)} %bitcast.86, bf16[128,1536]{0,1:T(8,128)(2,1)} %bitcast.82, bf16[3072,1536]{1,0:T(8,128)(2,1)S(1)} %bitcast.77), kind=kOutput, calls=%fused_computation.13 | convolution fusion | flops 1209922560 | bytes 11427840 | tf_op jit(solution)/shard_map/dot_general | solution.py:123
  215.3 51.5 %all-reduce.2 = f32[3072]{0:T(1024)S(1)} all-reduce(f32[3072]{0:T(1024)S(1)} %get-tuple-element.7), channel_id=5, replica_groups=mesh['dp'=8,'seq'=16] {'seq'}, use_global_device_ids=true, to_apply=%region_9.10.clone | all-reduce | flops 3072 | bytes 24576
  266.8 0.6 dynamic-slice.3
  267.5 1.4 fusion.37
  268.9 169.7 %reduce-scatter.5.cloned.1.call-done = f32[24,1536]{1,0:T(8,128)} async-done(((f32[3072,1536]{1,0:T(8,128)}), f32[24,1536]{1,0:T(8,128)}) %reduce-scatter.5.cloned.1.call-update) | async-done | bytes 147472 | tf_op jit(solution)/shard_map/reduce_scatter | solution.py:134
  438.6 0.0 copy-done.1
  (13 shorter events, 0.1 us)
Async XLA Ops:
  7.2 3.9 copy-start
  7.2 74.1 %copy-start.9 = (s32[1,128]{1,0:T(1,128)S(1)}, s32[1,128]{1,0:T(1,128)}, u32[]{:S(2)}) copy-start(s32[1,128]{1,0:T(1,128)} %param.17) | copy-start | bytes 1540
  7.2 73.2 %copy-start.7 = (bf16[1,128,1536]{2,1,0:T(8,128)(2,1)S(1)}, bf16[1,128,1536]{2,1,0:T(8,128)(2,1)}, u32[]{:S(2)}) copy-start(bf16[1,128,1536]{2,1,0:T(8,128)(2,1)} %param.22) | copy-start | bytes 1179652
  7.2 74.3 %copy-start.8 = (bf16[1,128,1536]{2,1,0:T(8,128)(2,1)S(1)}, bf16[1,128,1536]{2,1,0:T(8,128)(2,1)}, u32[]{:S(2)}) copy-start(bf16[1,128,1536]{2,1,0:T(8,128)(2,1)} %param.20) | copy-start | bytes 1179652
  7.2 70.1 %reduce-scatter.3.cloned.1.call-start = ((), (), s32[]{:S(2)}) async-start(), calls=%async_computation.2 | async-start | bytes 2506752 | tf_op jit(solution)/shard_map/reduce_scatter | solution.py:91
  13.7 113.4 %all-gather.3.cloned.1.call-start = ((), (), s32[]{:S(2)}) async-start(), calls=%async_computation.3 | async-start | bytes 7102464 | tf_op jit(solution)/shard_map/all_gather | solution.py:111
  80.3 94.2 %all-gather.5.cloned.1.call-start = ((), (), s32[]{:S(2)}) async-start(), calls=%async_computation.4 | async-start | bytes 7102464 | tf_op jit(solution)/shard_map/all_gather | solution.py:112
  81.2 357.4 %reduce-scatter.5.cloned.1.call-start = ((), (), s32[]{:S(2)}) async-start(), calls=%async_computation.5 | async-start | bytes 19021824 | tf_op jit(solution)/shard_map/reduce_scatter | solution.py:134
  141.2 5.1 %copy-start.2 = (f32[12,136,2176]{2,1,0:T(8,128)}, f32[12,136,2176]{2,1,0:T(8,128)S(1)}, u32[]{:S(2)}) copy-start(f32[12,136,2176]{2,1,0:T(8,128)S(1)} %get-tuple-element.14) | copy-start | bytes 42614788
  183.9 10.7 %copy-start.3 = (bf16[1,128,3072]{2,1,0:T(8,128)(2,1)S(1)}, bf16[1,128,3072]{2,1,0:T(8,128)(2,1)}, u32[]{:S(2)}) copy-start(bf16[1,128,3072]{2,1,0:T(8,128)(2,1)} %param.25) | copy-start | bytes 2359300
  183.9 10.7 %copy-start.6 = (f32[1,3072]{1,0:T(1,128)S(1)}, f32[1,3072]{1,0:T(1,128)}, u32[]{:S(2)}) copy-start(f32[1,3072]{1,0:T(1,128)} %param.24) | copy-start | bytes 36868
  194.3 8.3 %copy-start.5 = (bf16[136,12,128]{2,0,1:T(8,128)(2,1)}, bf16[136,12,128]{2,0,1:T(8,128)(2,1)S(1)}, u32[]{:S(2)}) copy-start(bf16[136,12,128]{2,0,1:T(8,128)(2,1)S(1)} %fusion.15) | copy-start | bytes 1253380
  194.6 8.1 %copy-start.4 = (bf16[128,12,128]{0,2,1:T(8,128)(2,1)}, bf16[128,12,128]{0,2,1:T(8,128)(2,1)S(1)}, u32[]{:S(2)}) copy-start(bf16[128,12,128]{0,2,1:T(8,128)(2,1)S(1)} %copy.33) | copy-start | bytes 1179652
  202.7 7.1 %slice-start = ((s8[9437184]{0:T(1024)(128)(4,1)}), s8[1048576]{0:T(1024)(128)(4,1)S(1)}, s32[]{:S(2)}) async-start(s8[9437184]{0:T(1024)(128)(4,1)} %bitcast.76), calls=%async_computation.6 | async-start | bytes 2097152
  203.5 6.2 %slice-start.1 = ((s8[9437184]{0:T(1024)(128)(4,1)}), s8[4194304]{0:T(1024)(128)(4,1)S(1)}, s32[]{:S(2)}) async-start(s8[9437184]{0:T(1024)(128)(4,1)} %bitcast.76), calls=%async_computation.7 | async-start | bytes 8388608
  203.5 6.4 %slice-start.2 = ((s8[9437184]{0:T(1024)(128)(4,1)}), s8[4194304]{0:T(1024)(128)(4,1)S(1)}, s32[]{:S(2)}) async-start(s8[9437184]{0:T(1024)(128)(4,1)} %bitcast.76), calls=%async_computation.8 | async-start | bytes 8388608
  203.5 235.0 %copy-start.1 = (bf16[256,4608]{1,0:T(8,128)(2,1)S(1)}, bf16[256,4608]{1,0:T(8,128)(2,1)}, u32[]{:S(2)}) copy-start(bf16[256,4608]{1,0:T(8,128)(2,1)} %param.15) | copy-start | bytes 7077892
Sparse Core Ops, SparseCore 0:
  13.9 63.3 reduce-scatter.2
  80.4 46.6 all-gather.2
  129.4 45.1 all-gather.4
  202.8 235.6 reduce-scatter.4
where the time goes:
time: 447 us; the launch traced here: 445 us
  waiting for transfers between devices  271 us (61%)
  blocking collectives  80.8 us (18%)
  matrix products  37.4 us (8%)
  local copies, waits for them, and re-layouts  29.2 us (7%)
  between operations  16.2 us (4%)
  other arithmetic  10.6 us (2%)
    reduce_scatter x1, waiting for transfers between devices, on_device(): lax.psum_scatter(lax.dot_general(gated_grad, image_attn, (((0,), (0,)), (...  170 us
    unnamed x2, blocking collectives  80.8 us
    all_gather x1, waiting for transfers between devices, on_device(): lax.all_gather(key_rows, 'seq', axis=0, tiled=True)  45.1 us
    reduce_scatter x1, waiting for transfers between devices, on_device(): lax.psum_scatter(partial_proj, 'seq', scatter_dimension=0, tiled=True)  31.3 us
    all_gather x1, waiting for transfers between devices, on_device(): lax.all_gather(value_rows, 'seq', axis=0, tiled=True)  24.5 us
    dot_general x1, matrix products, attend(): jnp.einsum('hqk,khd->hqd', weights_now.astype(jnp.bfloat16), value_heads,...  10.4 us
    all_gather x1, local copies, waits for them, and re-layouts, on_device(): lax.all_gather(value_rows, 'seq', axis=0, tiled=True)  9.37 us
    all_gather x1, local copies, waits for them, and re-layouts, on_device(): lax.all_gather(key_rows, 'seq', axis=0, tiled=True)  9.33 us
  transfers between devices with their start and end apart: 4, of which 4 were waited for; matrix products, arithmetic and copies ran while one was open for 8% of the time, Pallas kernels for 0%

commit v1 on v0

v1 whole, which is shorter than its diff:
```python
import functools
import math

import jax
import jax.numpy as jnp
from jax import lax
from jax.experimental import pallas as pl
from jax.experimental.pallas import tpu as pltpu
from jax.sharding import PartitionSpec as P

EPS = 1e-06
NEG_BIG = -1e30
NY, NZ, NC = 2, 4, 2
NQ = NY * NC
F32 = jnp.float32
BF16 = jnp.bfloat16
NT = (((1,), (1,)), ((), ()))


def joint_kernel(
    n_dp,
    states_ref,
    gain_ref,
    text_proj_hbm,
    src_col_ref,
    src_row_ref,
    clen_ref,
    qgain_ref,
    kgain_ref,
    q_hbm,
    k_hbm,
    v_hbm,
    wo_hbm,
    gate_ref,
    dout_hbm,
    image_out_ref,
    text_attn_ref,
    d_attn_ref,
    grad_wo_ref,
    grad_gate_ref,
    tp,
    wo,
    dout,
    part,
    tbuf,
    qi,
    qt,
    kv,
    g,
    gtf,
    gt,
    gt_all,
    a_all,
    a_rows,
    tsend,
    trecv,
    psend,
    precv,
    fsend,
    fin,
    gsend,
    grecv,
    load_sem,
    loc_sem,
    kvq_s,
    kvq_r,
    fwd_s,
    fwd_r,
    txp_s,
    txp_r,
    txkv_s,
    txkv_r,
    g1_s,
    g1_r,
    gz_s,
    gz_r,
    aret_s,
    aret_r,
    tret_s,
    tret_r,
    apl_s,
    apl_r,
    dp_s,
    dp_r,
    fin_s,
    fin_r,
    gg_s,
    gg_r,
):
    dp = lax.axis_index("dp")
    me = lax.axis_index("seq")
    n_seq = NY * NZ * NC
    y = me // (NZ * NC)
    z = (me // NC) % NZ
    c = me % NC
    q = y * NC + c
    rows, inner = a_rows.shape[1], NZ * a_rows.shape[2]
    hg = a_rows.shape[2]
    head = 128
    n_heads = hg // head
    d_model = dout.shape[1]
    slots = src_row_ref.shape[1]
    tq = slots // NQ
    ts = tq // NZ
    image_keys = n_seq * rows
    blk = gt.shape[2]
    piece = blk // NZ

    def at_z(z_to):
        return y * (NZ * NC) + z_to * NC + c

    s_y = (1 - y) * (NZ * NC) + z * NC + c
    s_c = y * (NZ * NC) + z * NC + (1 - c)
    s_d = (1 - y) * (NZ * NC) + z * NC + (1 - c)
    q_y = (1 - y) * NC + c
    q_c = y * NC + (1 - c)
    q_d = (1 - y) * NC + (1 - c)

    def to_seq(src, dst, ss, rs, target):
        return pltpu.make_async_remote_copy(
            src_ref=src,
            dst_ref=dst,
            send_sem=ss,
            recv_sem=rs,
            device_id={"seq": target},
            device_id_type=pl.DeviceIdType.MESH,
        )

    load_tp = pltpu.make_async_copy(text_proj_hbm, tp, load_sem.at[0])
    load_dout = pltpu.make_async_copy(dout_hbm, dout, load_sem.at[1])
    load_wo = pltpu.make_async_copy(wo_hbm, wo, load_sem.at[2])
    load_tp.start()
    load_dout.start()
    load_wo.start()

    def col(index):
        return pl.ds(pl.multiple_of(index * hg, 128), hg)

    def kv_rows(q_from, z_from):
        return pl.ds(pl.multiple_of((q_from * NZ + z_from) * rows, 128), rows)

    own_rows = kv_rows(q, z)
    own = [
        pltpu.make_async_copy(k_hbm.at[:, col(z)], kv.at[0, own_rows, :], loc_sem.at[0]),
        pltpu.make_async_copy(v_hbm.at[:, col(z)], kv.at[1, own_rows, :], loc_sem.at[1]),
        pltpu.make_async_copy(q_hbm.at[:, col(z)], qi.at[z], loc_sem.at[2]),
    ]
    for copy in own:
        copy.start()

    barrier = pltpu.get_barrier_semaphore()

    @pl.loop(1, n_seq)
    def _(offset):
        pl.semaphore_signal(
            barrier,
            inc=1,
            device_id={"seq": (me + offset) % n_seq},
            device_id_type=pl.DeviceIdType.MESH,
        )

    @pl.loop(1, n_dp)
    def _(offset):
        pl.semaphore_signal(
            barrier,
            inc=1,
            device_id={"dp": (dp + offset) % n_dp},
            device_id_type=pl.DeviceIdType.MESH,
        )

    pl.semaphore_wait(barrier, n_seq - 1 + n_dp - 1)

    kvq = {}
    for dz in (2, 1, 3):
        z_to = (z + dz) % NZ
        target = at_z(z_to)
        kvq[dz] = (
            to_seq(k_hbm.at[:, col(z_to)], kv.at[0, own_rows, :], kvq_s.at[0, dz - 1], kvq_r.at[0, dz - 1], target),
            to_seq(v_hbm.at[:, col(z_to)], kv.at[1, own_rows, :], kvq_s.at[1, dz - 1], kvq_r.at[1, dz - 1], target),
            to_seq(q_hbm.at[:, col(z_to)], qi.at[z], kvq_s.at[2, dz - 1], kvq_r.at[2, dz - 1], target),
        )
        kvq[dz][0].start()
        kvq[dz][1].start()
    for dz in (2, 1, 3):
        kvq[dz][2].start()

    lane = lax.broadcasted_iota(jnp.int32, (slots, slots), 1)
    onehot = jnp.where(src_col_ref[...] == lane, 1.0, 0.0).astype(BF16)
    picked = jnp.dot(onehot, states_ref[...], preferred_element_type=F32)
    scaled = (picked * gain_ref[...]).astype(BF16)
    squares = jnp.sum(picked * picked, axis=1, keepdims=True)
    squares_high = squares.astype(BF16)
    squares_low = (squares - squares_high.astype(F32)).astype(BF16)
    tail_lane = lax.broadcasted_iota(jnp.int32, (slots, 128), 1)
    tail = jnp.where(tail_lane < 64, squares_high.astype(F32), squares_low.astype(F32)).astype(BF16)
    load_tp.wait()
    for zz in range(NZ):
        for kind in range(3):
            block = jnp.dot(
                scaled,
                tp[:, kind * inner + zz * hg : kind * inner + (zz + 1) * hg],
                preferred_element_type=F32,
            )
            part[zz, :, kind * hg : (kind + 1) * hg] = block.astype(BF16)
        part[zz, :, 3 * hg : 3 * hg + 128] = tail

    def text_copy(offset):
        target = (me + offset) % n_seq
        z_to = (target // NC) % NZ
        q_to = (target // (NZ * NC)) * NC + target % NC
        return to_seq(
            part.at[z_to, pl.ds(pl.multiple_of(q_to * tq, 32), tq), :],
            tbuf.at[offset - 1],
            txp_s.at[offset - 1],
            txp_r.at[offset - 1],
            target,
        )

    @pl.loop(1, n_seq)
    def _(offset):
        text_copy(offset).start()

    load_dout.wait()
    for t in range(d_model // 128):
        cols = slice(t * 128, (t + 1) * 128)
        gated = gate_ref[:, cols] * dout[:, cols].astype(F32)
        g[:, cols] = gated.astype(BF16)
        gtf[cols, :] = jnp.transpose(gated)
    for p in range(n_dp):
        for qq in range(NQ):
            pieces = []
            for zz in range(NZ):
                owner = (qq // NC) * (NZ * NC) + zz * NC + qq % NC
                start = (p * n_seq + owner) * piece
                pieces.append(gtf[start : start + piece, :])
            gt[qq, p] = jnp.concatenate(pieces, axis=0).astype(BF16)

    def gcols(q_from, z_from):
        return pl.ds(pl.multiple_of((q_from * NZ + z_from) * rows, 128), rows)

    g1 = []
    for i, (q_to, target) in enumerate(((q_y, s_y), (q_c, s_c), (q_d, s_d))):
        copy = to_seq(gt.at[q_to], gt_all.at[:, :, gcols(q, z)], g1_s.at[i], g1_r.at[i], target)
        copy.start()
        g1.append(copy)
    own_g = pltpu.make_async_copy(gt.at[q], gt_all.at[:, :, gcols(q, z)], loc_sem.at[3])
    own_g.start()

    def forward(dz):
        block = kv.at[:, kv_rows(q, (z - dz + NZ) % NZ), :]
        return (
            to_seq(block, block, fwd_s.at[0, dz], fwd_r.at[0, dz], s_y),
            to_seq(block, block, fwd_s.at[1, dz], fwd_r.at[1, dz], s_c),
        )

    def relay(dz):
        block = kv.at[:, kv_rows(q_y, (z - dz + NZ) % NZ), :]
        return to_seq(block, block, fwd_s.at[2, dz], fwd_r.at[2, dz], s_c)

    own[0].wait()
    own[1].wait()
    for dz in (0, 1, 3, 2):
        if dz:
            kvq[dz][0].wait_recv()
            kvq[dz][1].wait_recv()
        for copy in forward(dz):
            copy.start()

    ahead = 1 - 2 * c
    z_p = (z + ahead + NZ) % NZ
    z_n = (z - ahead + NZ) % NZ

    def g_ahead(i, q_from):
        block = gt_all.at[:, :, gcols(q_from, z)]
        return (
            to_seq(block, block, gz_s.at[0, i], gz_r.at[0, i], at_z(z_p)),
            to_seq(block, block, gz_s.at[1, i], gz_r.at[1, i], at_z(z_n)),
        )

    def g_relay(i, q_from):
        block = gt_all.at[:, :, gcols(q_from, z_n)]
        return to_seq(block, block, gz_s.at[2, i], gz_r.at[2, i], at_z(z_p))

    own_g.wait()
    for copy in g_ahead(0, q):
        copy.start()

    load_wo.wait()
    for t in range(inner // 256):
        cols = slice(t * 256, (t + 1) * 256)
        d_attn_ref[:, cols] = jnp.dot(g[...], wo[:, cols], preferred_element_type=F32).astype(BF16)

    for dz in (0, 1, 3, 2):
        forward(dz)[0].wait_recv()
        relay(dz).start()

    def add_part(offset, total):
        text_copy(offset).wait_recv()
        return total + tbuf[offset - 1].astype(F32)

    own_slots = pl.ds(pl.multiple_of(q * tq, 32), tq)
    total = part[z, own_slots, :].astype(F32)
    total = lax.fori_loop(1, n_seq, add_part, total)
    square_sum = total[:, 3 * hg : 3 * hg + 1] + total[:, 3 * hg + 64 : 3 * hg + 65]
    rate = lax.rsqrt(square_sum / (n_seq * states_ref.shape[1]) + EPS)
    normed = total[:, : 3 * hg] * rate
    text_rows = pl.ds(pl.multiple_of(image_keys + q * tq, 32), tq)
    for h in range(n_heads):
        for kind, gains in ((0, qgain_ref), (1, kgain_ref)):
            x = normed[:, kind * hg + h * head : kind * hg + (h + 1) * head]
            x = x * lax.rsqrt(jnp.mean(x * x, axis=1, keepdims=True) + EPS) * gains[...]
            if kind == 0:
                qt[:, h * head : (h + 1) * head] = x.astype(BF16)
            else:
                kv[0, text_rows, h * head : (h + 1) * head] = x.astype(BF16)
    kv[1, text_rows, :] = normed[:, 2 * hg : 3 * hg].astype(BF16)
    text_block = kv.at[:, text_rows, :]
    txkv = []
    for i, target in enumerate((s_y, s_c, s_d)):
        copy = to_seq(text_block, text_block, txkv_s.at[i], txkv_r.at[i], target)
        copy.start()
        txkv.append(copy)

    for i, q_from in ((1, q_y), (2, q_c), (3, q_d)):
        g1[i - 1].wait_recv()
        for copy in g_ahead(i, q_from):
            copy.start()

    own[2].wait()
    for dz in (1, 3, 2):
        kvq[dz][2].wait_recv()
    for dz in (0, 1, 3, 2):
        forward(dz)[1].wait_recv()
        relay(dz).wait_recv()
    for copy in txkv:
        copy.wait_recv()

    factor = head ** (-0.5) * math.log2(math.e)
    bias = jnp.where(src_row_ref[...] < clen_ref[0], 0.0, NEG_BIG)

    def attend(query, h):
        cols = slice(h * head, (h + 1) * head)
        image_scores = lax.dot_general(query, kv[0, :image_keys, cols], NT, preferred_element_type=F32)
        text_scores = lax.dot_general(query, kv[0, image_keys:, cols], NT, preferred_element_type=F32) + bias
        top = jnp.maximum(
            jnp.max(image_scores, axis=1, keepdims=True), jnp.max(text_scores, axis=1, keepdims=True)
        )
        image_probs = jnp.exp2((image_scores - top) * factor)
        text_probs = jnp.exp2((text_scores - top) * factor)
        denom = jnp.sum(image_probs, axis=1, keepdims=True) + jnp.sum(text_probs, axis=1, keepdims=True)
        summed = jnp.dot(image_probs.astype(BF16), kv[1, :image_keys, cols], preferred_element_type=F32)
        summed += jnp.dot(text_probs.astype(BF16), kv[1, image_keys:, cols], preferred_element_type=F32)
        return summed / denom

    def a_block(q_from, z_of):
        return a_all.at[kv_rows(q_from, z_of), :]

    def a_return(i):
        z_to = (z + i + 1) % NZ
        return to_seq(a_block(q, z_to), a_rows.at[z], aret_s.at[i], aret_r.at[i], at_z(z_to))

    def a_plane(i):
        block = a_block(q, (z + i + 1) % NZ)
        return (
            to_seq(block, block, apl_s.at[0, i], apl_r.at[0, i], s_y),
            to_seq(block, block, apl_s.at[1, i], apl_r.at[1, i], s_c),
        )

    def a_relay(i):
        block = a_block(q_y, (z + i + 1) % NZ)
        return to_seq(block, block, apl_s.at[2, i], apl_r.at[2, i], s_c)

    def g_source(i):
        y_from = (y + i % 2) % NY
        c_from = (c + i // 2) % NC
        return y_from * NC + c_from

    @pl.loop(0, NZ)
    def _(i):
        z_to = (z + i + 1) % NZ
        for h in range(n_heads):
            cols = slice(h * head, (h + 1) * head)
            result = attend(qi[z_to, :, cols], h)
            a_all[kv_rows(q, z_to), cols] = result.astype(BF16)

        @pl.when(i < NZ - 1)
        def _():
            a_return(i).start()

        for copy in a_plane(i):
            copy.start()
        source = g_source(i)
        g_ahead(i, source)[0].wait_recv()
        g_relay(i, source).start()

    a_rows[z] = a_all[kv_rows(q, z), :]

    slot_valid = src_col_ref[own_slots, :] < clen_ref[0]
    for h in range(n_heads):
        cols = slice(h * head, (h + 1) * head)
        result = jnp.where(slot_valid, attend(qt[:, cols], h), 0.0)
        for zz in range(NZ):
            tsend[zz, :, cols] = result[zz * ts : (zz + 1) * ts, :]

    def t_return(dz):
        z_to = (z + dz) % NZ
        return to_seq(tsend.at[z_to], trecv.at[z], tret_s.at[dz - 1], tret_r.at[dz - 1], at_z(z_to))

    for dz in range(1, NZ):
        t_return(dz).start()
    trecv[z] = tsend[z]

    @pl.loop(0, NZ)
    def _(i):
        a_plane(i)[0].wait_recv()
        a_relay(i).start()

    @pl.loop(0, NZ)
    def _(i):
        source = g_source(i)
        g_ahead(i, source)[1].wait_recv()
        g_relay(i, source).wait_recv()
        a_plane(i)[1].wait_recv()

    @pl.loop(0, NZ)
    def _(i):
        a_relay(i).wait_recv()

    def grad_block(p):
        return jnp.dot(gt_all[p], a_all[...], preferred_element_type=F32)

    def dp_copy(j):
        p = (dp + 1 + j) % n_dp
        return pltpu.make_async_remote_copy(
            src_ref=psend.at[p],
            dst_ref=precv.at[j],
            send_sem=dp_s.at[j],
            recv_sem=dp_r.at[j],
            device_id={"dp": p},
            device_id_type=pl.DeviceIdType.MESH,
        )

    @pl.loop(0, n_dp - 1)
    def _(j):
        p = (dp + 1 + j) % n_dp
        psend[p] = grad_block(p).astype(BF16)
        dp_copy(j).start()

    own_grad = grad_block(dp)

    for i in range(NZ - 1):
        a_return(i).wait_recv()
    image_attn = jnp.concatenate([a_rows[zz] for zz in range(NZ)], axis=1)
    per = d_model // n_seq
    for t in range(n_seq // 2):
        cols = slice(t * 2 * per, (t + 1) * 2 * per)
        projected = lax.dot_general(image_attn, wo[cols, :], NT, preferred_element_type=F32)
        image_out_ref[:, cols] = (gate_ref[:, cols] * projected).astype(BF16)
        term = jnp.sum(projected * dout[:, cols].astype(F32), axis=0, keepdims=True)
        gsend[2 * t, :, :per] = jnp.broadcast_to(term[:, :per], (8, per))
        gsend[2 * t + 1, :, :per] = jnp.broadcast_to(term[:, per:], (8, per))

    def gate_copy(offset):
        target = (me + offset) % n_seq
        return to_seq(gsend.at[target], grecv.at[offset - 1], gg_s.at[offset - 1], gg_r.at[offset - 1], target)

    @pl.loop(1, n_seq)
    def _(offset):
        gate_copy(offset).start()

    def add_grad(j, total):
        dp_copy(j).wait_recv()
        return total + precv[j].astype(F32)

    grad = lax.fori_loop(0, n_dp - 1, add_grad, own_grad)
    for zz in range(NZ):
        fsend[zz] = grad[zz * piece : (zz + 1) * piece, :]

    def final_copy(dz):
        z_to = (z + dz) % NZ
        return to_seq(fsend.at[z_to], fin.at[z], fin_s.at[dz - 1], fin_r.at[dz - 1], at_z(z_to))

    for dz in range(1, NZ):
        final_copy(dz).start()
    fin[z] = fsend[z]

    for dz in range(1, NZ):
        t_return(dz).wait_recv()
    for zz in range(NZ):
        text_attn_ref[:, zz * hg : (zz + 1) * hg] = trecv[zz].astype(BF16)

    def add_gate(offset, total):
        gate_copy(offset).wait_recv()
        return total + grecv[offset - 1]

    gate_total = lax.fori_loop(1, n_seq, add_gate, gsend[me])
    grad_gate_ref[...] = gate_total[0:1, :per]

    for dz in range(1, NZ):
        final_copy(dz).wait_recv()
    for zz in range(NZ):
        grad_wo_ref[:, zz * hg : (zz + 1) * hg] = fin[zz]

    for dz in range(1, NZ):
        for copy in kvq[dz]:
            copy.wait_send()
        t_return(dz).wait_send()
        final_copy(dz).wait_send()
        a_return(dz - 1).wait_send()
    for copy in g1 + txkv:
        copy.wait_send()

    @pl.loop(0, NZ)
    def _(i):
        source = g_source(i)
        for copy in (*forward(i), relay(i), *g_ahead(i, source), g_relay(i, source), *a_plane(i), a_relay(i)):
            copy.wait_send()

    @pl.loop(1, n_seq)
    def _(offset):
        text_copy(offset).wait_send()
        gate_copy(offset).wait_send()

    @pl.loop(0, n_dp - 1)
    def _(j):
        dp_copy(j).wait_send()


def on_device(
    n_dp,
    caption_states,
    caption_gain,
    text_proj,
    caption_len,
    slot_source,
    query_gain,
    key_gain,
    image_q,
    image_k,
    image_v,
    out_weight,
    gate,
    d_out,
):
    slots = slot_source.shape[1]
    rows, inner = image_q.shape[1:]
    d_model = d_out.shape[2]
    n_seq = NY * NZ * NC
    hg = inner // NZ
    tq = slots // NQ
    ts = tq // NZ
    blk = d_model // n_dp // NQ
    piece = blk // NZ
    per = d_model // n_seq
    sources = slot_source[0].reshape(NY, NZ, NC, ts).transpose(0, 2, 1, 3).reshape(slots)
    vmem = pl.BlockSpec(memory_space=pltpu.VMEM)
    hbm = pl.BlockSpec(memory_space=pl.ANY)
    smem = pl.BlockSpec(memory_space=pltpu.SMEM)
    dma = pltpu.SemaphoreType.DMA
    sems = [
        (3,), (4,), (3, 3), (3, 3), (3, NZ), (3, NZ), (n_seq - 1,), (n_seq - 1,), (3,), (3,), (3,), (3,),
        (3, NZ), (3, NZ), (3,), (3,), (3,), (3,), (3, NZ), (3, NZ), (n_dp - 1,), (n_dp - 1,), (3,), (3,),
        (n_seq - 1,), (n_seq - 1,),
    ]
    outs = pl.pallas_call(
        functools.partial(joint_kernel, n_dp),
        out_shape=(
            jax.ShapeDtypeStruct((rows, d_model), BF16),
            jax.ShapeDtypeStruct((ts, inner), BF16),
            jax.ShapeDtypeStruct((rows, inner), BF16),
            jax.ShapeDtypeStruct((piece, inner), F32),
            jax.ShapeDtypeStruct((1, per), F32),
        ),
        in_specs=[vmem, vmem, hbm, vmem, vmem, smem, vmem, vmem, hbm, hbm, hbm, hbm, vmem, hbm],
        out_specs=(vmem,) * 5,
        scratch_shapes=[
            pltpu.VMEM(text_proj.shape, BF16),
            pltpu.VMEM(out_weight.shape, BF16),
            pltpu.VMEM((rows, d_model), BF16),
            pltpu.VMEM((NZ, slots, 3 * hg + 128), BF16),
            pltpu.VMEM((n_seq - 1, tq, 3 * hg + 128), BF16),
            pltpu.VMEM((NZ, rows, hg), BF16),
            pltpu.VMEM((tq, hg), BF16),
            pltpu.VMEM((2, n_seq * rows + slots, hg), BF16),
            pltpu.VMEM((rows, d_model), BF16),
            pltpu.VMEM((d_model, rows), F32),
            pltpu.VMEM((NQ, n_dp, blk, rows), BF16),
            pltpu.VMEM((n_dp, blk, n_seq * rows), BF16),
            pltpu.VMEM((n_seq * rows, hg), BF16),
            pltpu.VMEM((NZ, rows, hg), BF16),
            pltpu.VMEM((NZ, ts, hg), F32),
            pltpu.VMEM((NZ, ts, hg), F32),
            pltpu.VMEM((n_dp, blk, hg), BF16),
            pltpu.VMEM((n_dp - 1, blk, hg), BF16),
            pltpu.VMEM((NZ, piece, hg), F32),
            pltpu.VMEM((NZ, piece, hg), F32),
            pltpu.VMEM((n_seq, 8, 256), F32),
            pltpu.VMEM((n_seq - 1, 8, 256), F32),
            *[dma(shape) for shape in sems],
        ],
        compiler_params=pltpu.CompilerParams(
            collective_id=0, has_side_effects=True, vmem_limit_bytes=58 * 1024 * 1024
        ),
        name="joint",
    )(
        caption_states[0],
        caption_gain[None],
        text_proj,
        sources[:, None],
        sources[None],
        caption_len,
        query_gain[None],
        key_gain[None],
        image_q[0],
        image_k[0],
        image_v[0],
        out_weight,
        gate,
        d_out[0],
    )
    image_out, text_attn, d_attn, grad_wo, grad_gate = outs
    return (image_out[None], text_attn[None], d_attn[None], grad_wo, grad_gate)


def solution(mesh):
    in_specs = (
        P("dp", None, "seq"),
        P("seq"),
        P("seq", None),
        P("dp"),
        P("dp", None),
        P(),
        P(),
        P("dp", "seq", None),
        P("dp", "seq", None),
        P("dp", "seq", None),
        P(),
        P("dp", None),
        P("dp", "seq", None),
    )
    out_specs = (
        P("dp", "seq", None),
        P("dp", "seq", None),
        P("dp", "seq", None),
        P(("dp", "seq"), None),
        P("dp", "seq"),
    )
    return jax.shard_map(
        functools.partial(on_device, mesh.shape["dp"]),
        mesh=mesh,
        in_specs=in_specs,
        out_specs=out_specs,
        check_vma=False,
    )
```

time: 447 us -> 113 us (0.25)
  waiting for transfers between devices: 271 us -> 0 us
  Pallas kernels: 0 us -> 99.7 us
  blocking collectives: 80.8 us -> 0 us
  matrix products: 37.4 us -> 0 us
  local copies, waits for them, and re-layouts: 29.2 us -> 9.91 us
  between operations: 16.2 us -> 1.3 us
  other arithmetic: 10.6 us -> 1.32 us
    reduce_scatter x2 -> x0, waiting for transfers between devices: 201 us -> none  [the longest x1 170 us: on_device(): lax.psum_scatter(lax.dot_general(gated_grad, image_attn, (((0,), (0,)), (...]
    pallas_call x0 -> x1, Pallas kernels: none -> 99.7 us  [on_device(): pl.pallas_call(functools.partial(joint_kernel, n_dp), out_shape=(jax.Shap...]
    unnamed x2 -> x0, blocking collectives: 80.8 us -> none
    all_gather x2 -> x0, waiting for transfers between devices: 69.6 us -> none  [the longest x1 45.1 us: on_device(): lax.all_gather(key_rows, 'seq', axis=0, tiled=True)]
    dot_general x6 -> x0, matrix products: 37.4 us -> none  [the longest x1 10.4 us: attend(): jnp.einsum('hqk,khd->hqd', weights_now.astype(jnp.bfloat16), value_heads,...]
    all_gather x2 -> x0, local copies, waits for them, and re-layouts: 18.7 us -> none  [the longest x1 9.37 us: on_device(): lax.all_gather(value_rows, 'seq', axis=0, tiled=True)]
  transfers between devices with their start and end apart: 4 -> 0, of which waited for: 4 -> 0; matrix products, arithmetic and copies ran while one was open for 8% -> 0% of each run, Pallas kernels for 0% -> 0%
where the time goes in v1:
time: 113 us; the launch traced here: 112 us
  Pallas kernels  99.7 us (88%)
  local copies, waits for them, and re-layouts  9.91 us (9%)
  other arithmetic  1.32 us (1%)
  between operations  1.3 us (1%)
    pallas_call x1, Pallas kernels, on_device(): pl.pallas_call(functools.partial(joint_kernel, n_dp), out_shape=(jax.Shap...  99.7 us
    unnamed x6, local copies, waits for them, and re-layouts  8.49 us

profile of v1, /device:TPU:1, one launch (start us, length us, event | category | flops | bytes accessed | tf_op | source)
XLA Modules:
  0.0 112.3 jit_solution(11337117899329638512)
XLA Ops:
  1.3 0.5 broadcast.3
  1.8 1.3 %reduce.3 = s32[128]{0:T(128)S(1)} reduce(s32[1,128]{1,0:T(1,128)} %param.17, s32[]{:T(128)} %broadcast.3), dimensions={0}, to_apply=%param.17.reduce_sub_computation.3 | reduce | bytes 1028 | tf_op args[4]
  3.1 0.1 reshape_squeeze.3
  3.2 0.6 broadcast_in_dim_reshape.7.src_row_ref
  3.8 0.7 broadcast_in_dim_reshape.8.src_col_ref
  4.5 99.7 %joint.1 = (bf16[128,3072]{1,0:T(8,128)(2,1)}, bf16[8,1536]{1,0:T(8,128)(2,1)}, bf16[128,1536]{1,0:T(8,128)(2,1)}, f32[24,1536]{1,0:T(8,128)}, f32[1,192]{1,0:T(1,128)}) custom-call(bf16[128,256]{1,0:T(8,128)(2,1)} %bitcast.18, f32[1,256]{1,0:T(1,128)} %bitcast.21, bf16[256,4608]{1,0:T(8,128)(2,1)} %text_proj_hbm.1, ...), custom_call_target="tpu_custom_call" | custom-call | tf_op jit(solution)/shard_map/joint/pallas_call | solution.py:565
  104.3 2.1 %copy.27 = bf16[1,128,3072]{2,1,0:T(8,128)(2,1)} copy(bf16[1,128,3072]{2,1,0:T(8,128)(2,1)} %bitcast.13) | data formatting | bytes 1572864
  106.4 1.3 %copy.28 = bf16[1,8,1536]{2,1,0:T(8,128)(2,1)} copy(bf16[1,8,1536]{2,1,0:T(8,128)(2,1)} %bitcast.20) | data formatting | bytes 49152
  107.7 1.8 %copy.29 = bf16[1,128,1536]{2,1,0:T(8,128)(2,1)} copy(bf16[1,128,1536]{2,1,0:T(8,128)(2,1)} %bitcast.17) | data formatting | bytes 786432
  109.5 1.6 %copy.30 = f32[24,1536]{1,0:T(8,128)} copy(f32[24,1536]{1,0:T(8,128)} %get-tuple-element.23) | data formatting | bytes 294912
  111.0 1.2 %copy.31 = f32[1,192]{1,0:T(1,128)} copy(f32[1,192]{1,0:T(1,128)} %get-tuple-element.24) | data formatting | bytes 1536
  (1 shorter events, 0.0 us)

commit v2 on v1

v2 whole, which is shorter than its diff:
```python
import functools
import math

import jax
import jax.numpy as jnp
from jax import lax
from jax.experimental import pallas as pl
from jax.experimental.pallas import tpu as pltpu
from jax.sharding import PartitionSpec as P

EPS = 1e-06
NEG_BIG = -1e30
NY, NZ, NC = 2, 4, 2
NQ = NY * NC
F32 = jnp.float32
BF16 = jnp.bfloat16
NT = (((1,), (1,)), ((), ()))


def joint_kernel(
    n_dp,
    states_ref,
    gain_ref,
    text_proj_hbm,
    source_ref,
    length_ref,
    qgain_ref,
    kgain_ref,
    q_hbm,
    k_hbm,
    v_hbm,
    wo_hbm,
    gate_ref,
    dout_hbm,
    image_out_ref,
    text_attn_ref,
    d_attn_ref,
    grad_wo_ref,
    grad_gate_ref,
    tp,
    wo,
    dout,
    part,
    core_recv,
    ysend_q,
    ysend_kv,
    yrecv_q,
    yrecv_kv,
    zsend_q,
    zsend_kv,
    zrecv_q,
    zrecv_kv,
    sq_send,
    sq_recv,
    sq_col,
    src_col,
    qi,
    qt,
    near_top,
    near_sum,
    near_acc,
    kv,
    g,
    gtf,
    gt,
    gt_all,
    a_all,
    a_rows,
    tsend,
    trecv,
    psend,
    precv,
    own_grad,
    fin,
    gsend,
    grecv,
    load_sem,
    loc_sem,
    kvq_s,
    kvq_r,
    fwd_s,
    fwd_r,
    core_s,
    core_r,
    ytx_s,
    ytx_r,
    ztx_s,
    ztx_r,
    sq_s,
    sq_r,
    txkv_s,
    txkv_r,
    g1_s,
    g1_r,
    gz_s,
    gz_r,
    aret_s,
    aret_r,
    tret_s,
    tret_r,
    apl_s,
    apl_r,
    dp_s,
    dp_r,
    gg_s,
    gg_r,
):
    dp = lax.axis_index("dp")
    me = lax.axis_index("seq")
    n_seq = NY * NZ * NC
    y = me // (NZ * NC)
    z = (me // NC) % NZ
    c = me % NC
    q = y * NC + c
    rows, inner = a_rows.shape[1], NZ * a_rows.shape[2]
    hg = a_rows.shape[2]
    head = 128
    n_heads = hg // head
    d_model = dout.shape[1]
    slots = source_ref.shape[1]
    tq = slots // NQ
    ts = tq // NZ
    image_keys = n_seq * rows
    blk = gt.shape[2]
    piece = blk // NZ

    def at_z(z_to):
        return y * (NZ * NC) + z_to * NC + c

    s_y = (1 - y) * (NZ * NC) + z * NC + c
    s_c = y * (NZ * NC) + z * NC + (1 - c)
    s_d = (1 - y) * (NZ * NC) + z * NC + (1 - c)
    q_y = (1 - y) * NC + c
    q_c = y * NC + (1 - c)
    q_d = (1 - y) * NC + (1 - c)

    def to_seq(src, dst, ss, rs, target):
        return pltpu.make_async_remote_copy(
            src_ref=src,
            dst_ref=dst,
            send_sem=ss,
            recv_sem=rs,
            device_id={"seq": target},
            device_id_type=pl.DeviceIdType.MESH,
        )

    load_tp = pltpu.make_async_copy(text_proj_hbm, tp, load_sem.at[0])
    load_dout = pltpu.make_async_copy(dout_hbm, dout, load_sem.at[1])
    load_wo = pltpu.make_async_copy(wo_hbm, wo, load_sem.at[2])
    load_tp.start()
    load_dout.start()
    load_wo.start()

    def col(index):
        return pl.ds(pl.multiple_of(index * hg, 128), hg)

    def kv_rows(q_from, z_from):
        return pl.ds(pl.multiple_of((q_from * NZ + z_from) * rows, 128), rows)

    own_rows = kv_rows(q, z)
    own = [
        pltpu.make_async_copy(k_hbm.at[:, col(z)], kv.at[0, own_rows, :], loc_sem.at[0]),
        pltpu.make_async_copy(v_hbm.at[:, col(z)], kv.at[1, own_rows, :], loc_sem.at[1]),
        pltpu.make_async_copy(q_hbm.at[:, col(z)], qi.at[z], loc_sem.at[2]),
    ]
    for copy in own:
        copy.start()

    barrier = pltpu.get_barrier_semaphore()

    @pl.loop(1, n_seq)
    def _(offset):
        pl.semaphore_signal(
            barrier,
            inc=1,
            device_id={"seq": (me + offset) % n_seq},
            device_id_type=pl.DeviceIdType.MESH,
        )

    @pl.loop(1, n_dp)
    def _(offset):
        for z_to in range(NZ):
            pl.semaphore_signal(
                barrier,
                inc=1,
                device_id={"dp": (dp + offset) % n_dp, "seq": at_z(z_to)},
                device_id_type=pl.DeviceIdType.MESH,
            )

    pl.semaphore_wait(barrier, n_seq - 1 + NZ * (n_dp - 1))

    kvq = {}
    for dz in (2, 1, 3):
        z_to = (z + dz) % NZ
        target = at_z(z_to)
        kvq[dz] = (
            to_seq(k_hbm.at[:, col(z_to)], kv.at[0, own_rows, :], kvq_s.at[0, dz - 1], kvq_r.at[0, dz - 1], target),
            to_seq(v_hbm.at[:, col(z_to)], kv.at[1, own_rows, :], kvq_s.at[1, dz - 1], kvq_r.at[1, dz - 1], target),
            to_seq(q_hbm.at[:, col(z_to)], qi.at[z], kvq_s.at[2, dz - 1], kvq_r.at[2, dz - 1], target),
        )
        kvq[dz][0].start()
        kvq[dz][1].start()
    for dz in (2, 1, 3):
        kvq[dz][2].start()

    def forward(dz):
        block = kv.at[:, kv_rows(q, (z - dz + NZ) % NZ), :]
        return (
            to_seq(block, block, fwd_s.at[0, dz], fwd_r.at[0, dz], s_y),
            to_seq(block, block, fwd_s.at[1, dz], fwd_r.at[1, dz], s_c),
        )

    def relay(dz):
        block = kv.at[:, kv_rows(q_y, (z - dz + NZ) % NZ), :]
        return to_seq(block, block, fwd_s.at[2, dz], fwd_r.at[2, dz], s_c)

    own[0].wait()
    own[1].wait()
    for copy in forward(0):
        copy.start()

    place = lax.broadcasted_iota(jnp.int32, (slots, slots), 0)
    lane = lax.broadcasted_iota(jnp.int32, (slots, slots), 1)
    at_c, at_y = place // (slots // NC), (place // tq) % NY
    slot_of = at_y * (slots // NY) + ((place // ts) % NZ) * (NC * ts) + at_c * ts + place % ts
    order = jnp.where(lane == slot_of, 1.0, 0.0).astype(BF16)
    row_at_slot = jnp.where(place == source_ref[...], 1.0, 0.0).astype(BF16)
    onehot = lax.dot_general(order, row_at_slot, NT, preferred_element_type=F32)
    src_col[...] = jnp.broadcast_to(
        jnp.sum(onehot * lane.astype(F32), axis=1, keepdims=True), (slots, slots)
    )
    onehot = onehot.astype(BF16)
    src_row = lax.dot_general(lane[:8].astype(F32).astype(BF16), onehot, NT, preferred_element_type=F32)
    picked = jnp.dot(onehot, states_ref[...], preferred_element_type=F32)
    scaled = (picked * gain_ref[...]).astype(BF16)
    squares = jnp.sum(picked * picked, axis=1, keepdims=True)
    sq_send[...] = jnp.transpose(jnp.broadcast_to(squares, (slots, slots)))[:8]

    load_tp.wait()
    for zz in range(NZ):
        for kind in range(3):
            block = jnp.dot(
                scaled,
                tp[:, kind * inner + zz * hg : kind * inner + (zz + 1) * hg],
                preferred_element_type=F32,
            )
            for i in range(NQ):
                part[i // NY, i % NY, zz, :, kind * hg : (kind + 1) * hg] = block[i * tq : (i + 1) * tq]

    core_copy = to_seq(part.at[1 - c], core_recv, core_s.at[0], core_r.at[0], s_c)
    core_copy.start()

    def square_copy(offset):
        target = (me + offset) % n_seq
        return to_seq(sq_send, sq_recv.at[offset - 1], sq_s.at[offset - 1], sq_r.at[offset - 1], target)

    @pl.loop(1, n_seq)
    def _(offset):
        square_copy(offset).start()

    load_dout.wait()
    for t in range(d_model // 128):
        cols = slice(t * 128, (t + 1) * 128)
        gated = gate_ref[:, cols] * dout[:, cols].astype(F32)
        g[:, cols] = gated.astype(BF16)
        gtf[cols, :] = jnp.transpose(gated)

    core_copy.wait_recv()
    for zz in range(NZ):
        summed = part[c, 1 - y, zz] + core_recv[1 - y, zz]
        ysend_q[zz] = summed[:, :hg]
        ysend_kv[zz] = summed[:, hg:].astype(BF16)
    y_copies = (
        to_seq(ysend_q, yrecv_q, ytx_s.at[0], ytx_r.at[0], s_y),
        to_seq(ysend_kv, yrecv_kv, ytx_s.at[1], ytx_r.at[1], s_y),
    )
    for copy in y_copies:
        copy.start()

    for p in range(n_dp):
        for qq in range(NQ):
            pieces = []
            for zz in range(NZ):
                owner = (qq // NC) * (NZ * NC) + zz * NC + qq % NC
                start = (p * n_seq + owner) * piece
                pieces.append(gtf[start : start + piece, :])
            gt[qq, p] = jnp.concatenate(pieces, axis=0).astype(BF16)

    def gcols(q_from, z_from):
        return pl.ds(pl.multiple_of((q_from * NZ + z_from) * rows, 128), rows)

    g1 = [
        to_seq(gt.at[q_to], gt_all.at[:, :, gcols(q, z)], g1_s.at[i], g1_r.at[i], target)
        for i, (q_to, target) in enumerate(((q_y, s_y), (q_c, s_c), (q_d, s_d)))
    ]
    g1[1].start()
    own_g = pltpu.make_async_copy(gt.at[q], gt_all.at[:, :, gcols(q, z)], loc_sem.at[3])
    own_g.start()

    ahead = 1 - 2 * c
    z_p = (z + ahead + NZ) % NZ
    z_n = (z - ahead + NZ) % NZ

    def g_ahead(i, q_from):
        block = gt_all.at[:, :, gcols(q_from, z)]
        return (
            to_seq(block, block, gz_s.at[0, i], gz_r.at[0, i], at_z(z_p)),
            to_seq(block, block, gz_s.at[1, i], gz_r.at[1, i], at_z(z_n)),
        )

    def g_relay(i, q_from):
        block = gt_all.at[:, :, gcols(q_from, z_n)]
        return to_seq(block, block, gz_s.at[2, i], gz_r.at[2, i], at_z(z_p))

    load_wo.wait()
    for t in range(inner // 256):
        cols = slice(t * 256, (t + 1) * 256)
        d_attn_ref[:, cols] = jnp.dot(g[...], wo[:, cols], preferred_element_type=F32).astype(BF16)

    for dz in (1, 3, 2):
        kvq[dz][0].wait_recv()
        kvq[dz][1].wait_recv()
        for copy in forward(dz):
            copy.start()

    for copy in y_copies:
        copy.wait_recv()
    for zz in range(NZ):
        summed = part[c, y, zz] + core_recv[y, zz]
        zsend_q[zz] = summed[:, :hg] + yrecv_q[zz]
        part[c, y, zz, :, hg:] = summed[:, hg:] + yrecv_kv[zz].astype(F32)
        zsend_kv[zz] = part[c, y, zz, :, hg:].astype(BF16)

    z_copies = []
    for dz in (2, 1, 3):
        z_to = (z + dz) % NZ
        for kind, (src, dst) in enumerate(((zsend_q, zrecv_q), (zsend_kv, zrecv_kv))):
            copy = to_seq(
                src.at[z_to], dst.at[dz - 1], ztx_s.at[kind, dz - 1], ztx_r.at[kind, dz - 1], at_z(z_to)
            )
            copy.start()
            z_copies.append(copy)

    own_g.wait()
    for copy in g_ahead(0, q):
        copy.start()
    g1[1].wait_recv()
    for copy in g_ahead(2, q_c):
        copy.start()

    own[2].wait()
    for dz in (1, 3, 2):
        kvq[dz][2].wait_recv()
    for dz in (0, 1, 3, 2):
        forward(dz)[1].wait_recv()

    factor = head ** (-0.5) * math.log2(math.e)
    half = image_keys // NY
    near_rows = pl.ds(pl.multiple_of(y * half, 128), half)
    far_rows = pl.ds(pl.multiple_of((1 - y) * half, 128), half)

    def attend_near(query, h):
        cols = slice(h * head, (h + 1) * head)
        scores = lax.dot_general(query, kv[0, near_rows, cols], NT, preferred_element_type=F32)
        top = jnp.max(scores, axis=1, keepdims=True)
        probs = jnp.exp2((scores - top) * factor)
        values = jnp.dot(probs.astype(BF16), kv[1, near_rows, cols], preferred_element_type=F32)
        return top, jnp.sum(probs, axis=1, keepdims=True), values

    for i in range(NZ):
        z_to = (z + i + 1) % NZ
        for h in range(n_heads):
            cols = slice(h * head, (h + 1) * head)
            top, total, values = attend_near(qi[z_to, :, cols], h)
            near_top[i, h] = jnp.broadcast_to(top, (rows, head))
            near_sum[i, h] = jnp.broadcast_to(total, (rows, head))
            near_acc[i, :, cols] = values
        dz = (0, 1, 3, 2)[i]
        forward(dz)[0].wait_recv()
        relay(dz).start()
        if i == 1:
            g1[0].start()
            g1[2].start()

    def add_square(offset, total):
        square_copy(offset).wait_recv()
        return total + sq_recv[offset - 1]

    square_row = lax.fori_loop(1, n_seq, add_square, sq_send[...])
    sq_col[...] = jnp.transpose(jnp.broadcast_to(square_row[0:1], (slots, slots)))
    own_slots = pl.ds(pl.multiple_of((c * NY + y) * tq, 32), tq)
    rate = lax.rsqrt(sq_col[own_slots, 0:1] / (n_seq * states_ref.shape[1]) + EPS)
    for copy in z_copies:
        copy.wait_recv()
    total_q = zsend_q[z]
    total_kv = part[c, y, z, :, hg:]
    for dz in range(1, NZ):
        total_q += zrecv_q[dz - 1]
        total_kv += zrecv_kv[dz - 1].astype(F32)
    normed_q, normed_kv = total_q * rate, total_kv * rate
    text_rows = pl.ds(pl.multiple_of(image_keys + (c * NY + y) * tq, 32), tq)
    for h in range(n_heads):
        cols = slice(h * head, (h + 1) * head)
        x = normed_q[:, cols]
        qt[:, cols] = (x * lax.rsqrt(jnp.mean(x * x, axis=1, keepdims=True) + EPS) * qgain_ref[...]).astype(BF16)
        x = normed_kv[:, cols]
        kv[0, text_rows, cols] = (
            x * lax.rsqrt(jnp.mean(x * x, axis=1, keepdims=True) + EPS) * kgain_ref[...]
        ).astype(BF16)
    kv[1, text_rows, :] = normed_kv[:, hg:].astype(BF16)
    text_block = kv.at[:, text_rows, :]
    txkv = []
    for i, target in enumerate((s_y, s_c, s_d)):
        copy = to_seq(text_block, text_block, txkv_s.at[i], txkv_r.at[i], target)
        copy.start()
        txkv.append(copy)

    for i, q_from in ((1, q_y), (3, q_d)):
        g1[i - 1].wait_recv()
        for copy in g_ahead(i, q_from):
            copy.start()
    for dz in (0, 1, 3, 2):
        relay(dz).wait_recv()
    for copy in txkv:
        copy.wait_recv()

    length = length_ref[...].astype(F32)
    bias = jnp.where(src_row[0:1] < length, 0.0, NEG_BIG)

    def attend(query, h, near):
        cols = slice(h * head, (h + 1) * head)
        near_max, near_total, near_values = near
        image_scores = lax.dot_general(query, kv[0, far_rows, cols], NT, preferred_element_type=F32)
        text_scores = lax.dot_general(query, kv[0, image_keys:, cols], NT, preferred_element_type=F32) + bias
        top = jnp.maximum(
            jnp.max(image_scores, axis=1, keepdims=True), jnp.max(text_scores, axis=1, keepdims=True)
        )
        top = jnp.maximum(top, near_max)
        image_probs = jnp.exp2((image_scores - top) * factor)
        text_probs = jnp.exp2((text_scores - top) * factor)
        scale = jnp.exp2((near_max - top) * factor)
        denom = jnp.sum(image_probs, axis=1, keepdims=True) + jnp.sum(text_probs, axis=1, keepdims=True)
        summed = jnp.dot(image_probs.astype(BF16), kv[1, far_rows, cols], preferred_element_type=F32)
        summed += jnp.dot(text_probs.astype(BF16), kv[1, image_keys:, cols], preferred_element_type=F32)
        return (summed + scale * near_values) / (denom + scale * near_total)

    def a_block(q_from, z_of):
        return a_all.at[kv_rows(q_from, z_of), :]

    def a_return(i):
        z_to = (z + i + 1) % NZ
        return to_seq(a_block(q, z_to), a_rows.at[z], aret_s.at[i], aret_r.at[i], at_z(z_to))

    def a_plane(i):
        block = a_block(q, (z + i + 1) % NZ)
        return (
            to_seq(block, block, apl_s.at[0, i], apl_r.at[0, i], s_y),
            to_seq(block, block, apl_s.at[1, i], apl_r.at[1, i], s_c),
        )

    def a_relay(i):
        block = a_block(q_y, (z + i + 1) % NZ)
        return to_seq(block, block, apl_s.at[2, i], apl_r.at[2, i], s_c)

    def g_source(i):
        y_from = (y + i % 2) % NY
        c_from = (c + i // 2) % NC
        return y_from * NC + c_from

    @pl.loop(0, NZ)
    def _(i):
        z_to = (z + i + 1) % NZ
        for h in range(n_heads):
            cols = slice(h * head, (h + 1) * head)
            near = near_top[i, h][:, :1], near_sum[i, h][:, :1], near_acc[i, :, cols]
            result = attend(qi[z_to, :, cols], h, near)
            a_all[kv_rows(q, z_to), cols] = result.astype(BF16)

        @pl.when(i < NZ - 1)
        def _():
            a_return(i).start()

        for copy in a_plane(i):
            copy.start()
        k = (i % 2) * 2 + i // 2
        source = g_source(k)
        g_ahead(k, source)[0].wait_recv()
        g_relay(k, source).start()

        @pl.when(i > 0)
        def _():
            a_plane(i - 1)[0].wait_recv()
            a_relay(i - 1).start()

    a_rows[z] = a_all[kv_rows(q, z), :]

    slot_valid = src_col[own_slots, 0:1] < length
    for h in range(n_heads):
        cols = slice(h * head, (h + 1) * head)
        result = jnp.where(slot_valid, attend(qt[:, cols], h, attend_near(qt[:, cols], h)), 0.0)
        for zz in range(NZ):
            tsend[zz, :, cols] = result[zz * ts : (zz + 1) * ts, :]

    def t_return(dz):
        z_to = (z + dz) % NZ
        return to_seq(tsend.at[z_to], trecv.at[z], tret_s.at[dz - 1], tret_r.at[dz - 1], at_z(z_to))

    for dz in range(1, NZ):
        t_return(dz).start()
    trecv[z] = tsend[z]

    a_plane(NZ - 1)[0].wait_recv()
    a_relay(NZ - 1).start()

    for i in range(NZ - 1):
        a_return(i).wait_recv()
    image_attn = jnp.concatenate([a_rows[zz] for zz in range(NZ)], axis=1)
    per = d_model // n_seq
    for t in range(n_seq // 2):
        cols = slice(t * 2 * per, (t + 1) * 2 * per)
        projected = lax.dot_general(image_attn, wo[cols, :], NT, preferred_element_type=F32)
        image_out_ref[:, cols] = (gate_ref[:, cols] * projected).astype(BF16)
        term = jnp.sum(projected * dout[:, cols].astype(F32), axis=0, keepdims=True)
        gsend[2 * t, :, :per] = jnp.broadcast_to(term[:, :per], (8, per))
        gsend[2 * t + 1, :, :per] = jnp.broadcast_to(term[:, per:], (8, per))

    def gate_copy(offset):
        target = (me + offset) % n_seq
        return to_seq(gsend.at[target], grecv.at[offset - 1], gg_s.at[offset - 1], gg_r.at[offset - 1], target)

    @pl.loop(1, n_seq)
    def _(offset):
        gate_copy(offset).start()

    @pl.loop(0, NZ)
    def _(i):
        source = g_source(i)
        g_ahead(i, source)[1].wait_recv()
        g_relay(i, source).wait_recv()
        a_plane(i)[1].wait_recv()
        a_relay(i).wait_recv()

    def grad_block(p):
        return jnp.dot(gt_all[p], a_all[...], preferred_element_type=F32)

    def dp_copy(jd, jz):
        p, z_to = (dp + jd) % n_dp, (z + jz) % NZ
        return pltpu.make_async_remote_copy(
            src_ref=psend.at[p, z_to],
            dst_ref=precv.at[jd, jz],
            send_sem=dp_s.at[jd, jz],
            recv_sem=dp_r.at[jd, jz],
            device_id={"dp": p, "seq": at_z(z_to)},
            device_id_type=pl.DeviceIdType.MESH,
        )

    @pl.loop(1, n_dp)
    def _(jd):
        p = (dp + jd) % n_dp
        block = grad_block(p)
        for zz in range(NZ):
            psend[p, zz] = block[zz * piece : (zz + 1) * piece].astype(BF16)
        for jz in range(NZ):
            dp_copy(jd, jz).start()

    block = grad_block(dp)
    for zz in range(NZ):
        own_grad[zz] = block[zz * piece : (zz + 1) * piece]
        psend[dp, zz] = block[zz * piece : (zz + 1) * piece].astype(BF16)
    for jz in range(1, NZ):
        dp_copy(0, jz).start()

    for dz in range(1, NZ):
        t_return(dz).wait_recv()
    for zz in range(NZ):
        text_attn_ref[:, zz * hg : (zz + 1) * hg] = trecv[zz].astype(BF16)

    def add_gate(offset, total):
        gate_copy(offset).wait_recv()
        return total + grecv[offset - 1]

    gate_total = lax.fori_loop(1, n_seq, add_gate, gsend[me])
    grad_gate_ref[...] = gate_total[0:1, :per]

    for jz in range(NZ):
        if jz:
            dp_copy(0, jz).wait_recv()
            first = precv[0, jz].astype(F32)
        else:
            first = own_grad[z]

        def add_grad(jd, total):
            dp_copy(jd, jz).wait_recv()
            return total + precv[jd, jz].astype(F32)

        fin[(z - jz + NZ) % NZ] = lax.fori_loop(1, n_dp, add_grad, first)
    for zz in range(NZ):
        grad_wo_ref[:, zz * hg : (zz + 1) * hg] = fin[zz]

    for dz in range(1, NZ):
        for copy in kvq[dz]:
            copy.wait_send()
        t_return(dz).wait_send()
        a_return(dz - 1).wait_send()
        dp_copy(0, dz).wait_send()
    for copy in (*g1, *txkv, *y_copies, *z_copies, core_copy):
        copy.wait_send()

    @pl.loop(0, NZ)
    def _(i):
        source = g_source(i)
        for copy in (*forward(i), relay(i), *g_ahead(i, source), g_relay(i, source), *a_plane(i), a_relay(i)):
            copy.wait_send()

    @pl.loop(1, n_seq)
    def _(offset):
        square_copy(offset).wait_send()
        gate_copy(offset).wait_send()

    @pl.loop(1, n_dp)
    def _(jd):
        for jz in range(NZ):
            dp_copy(jd, jz).wait_send()


def copy_out(*refs):
    sources, results, sem = refs[:5], refs[5:10], refs[10]
    copies = [
        pltpu.make_async_copy(src, dst, sem.at[i]) for i, (src, dst) in enumerate(zip(sources, results))
    ]
    for copy in copies:
        copy.start()
    for copy in copies:
        copy.wait()


def on_device(
    n_dp,
    caption_states,
    caption_gain,
    text_proj,
    caption_len,
    slot_source,
    query_gain,
    key_gain,
    image_q,
    image_k,
    image_v,
    out_weight,
    gate,
    d_out,
):
    slots = slot_source.shape[1]
    rows, inner = image_q.shape[1:]
    d_model = d_out.shape[2]
    n_seq = NY * NZ * NC
    hg = inner // NZ
    tq = slots // NQ
    ts = tq // NZ
    blk = d_model // n_dp // NQ
    piece = blk // NZ
    per = d_model // n_seq
    vmem = pl.BlockSpec(memory_space=pltpu.VMEM)
    hbm = pl.BlockSpec(memory_space=pl.ANY)
    dma = pltpu.SemaphoreType.DMA
    sems = [
        (3,), (4,), (3, 3), (3, 3), (3, NZ), (3, NZ), (1,), (1,), (2,), (2,), (2, 3), (2, 3), (n_seq - 1,),
        (n_seq - 1,), (3,), (3,), (3,), (3,), (3, NZ), (3, NZ), (3,), (3,), (3,), (3,), (3, NZ), (3, NZ),
        (n_dp, NZ), (n_dp, NZ), (n_seq - 1,), (n_seq - 1,),
    ]
    out_shape = (
        jax.ShapeDtypeStruct((rows, d_model), BF16),
        jax.ShapeDtypeStruct((ts, inner), BF16),
        jax.ShapeDtypeStruct((rows, inner), BF16),
        jax.ShapeDtypeStruct((piece, inner), F32),
        jax.ShapeDtypeStruct((1, per), F32),
    )
    outs = pl.pallas_call(
        functools.partial(joint_kernel, n_dp),
        out_shape=out_shape,
        in_specs=[vmem, vmem, hbm, vmem, vmem, vmem, vmem, hbm, hbm, hbm, hbm, vmem, hbm],
        out_specs=(vmem,) * 5,
        scratch_shapes=[
            pltpu.VMEM(text_proj.shape, BF16),
            pltpu.VMEM(out_weight.shape, BF16),
            pltpu.VMEM((rows, d_model), BF16),
            pltpu.VMEM((NC, NY, NZ, tq, 3 * hg), F32),
            pltpu.VMEM((NY, NZ, tq, 3 * hg), F32),
            *[pltpu.VMEM((n, tq, width), dtype) for n in (NZ, NZ, NZ, 3) for width, dtype in ((hg, F32), (2 * hg, BF16))],
            pltpu.VMEM((8, slots), F32),
            pltpu.VMEM((n_seq - 1, 8, slots), F32),
            pltpu.VMEM((slots, slots), F32),
            pltpu.VMEM((slots, slots), F32),
            pltpu.VMEM((NZ, rows, hg), BF16),
            pltpu.VMEM((tq, hg), BF16),
            pltpu.VMEM((NZ, hg // 128, rows, 128), F32),
            pltpu.VMEM((NZ, hg // 128, rows, 128), F32),
            pltpu.VMEM((NZ, rows, hg), F32),
            pltpu.VMEM((2, n_seq * rows + slots, hg), BF16),
            pltpu.VMEM((rows, d_model), BF16),
            pltpu.VMEM((d_model, rows), F32),
            pltpu.VMEM((NQ, n_dp, blk, rows), BF16),
            pltpu.VMEM((n_dp, blk, n_seq * rows), BF16),
            pltpu.VMEM((n_seq * rows, hg), BF16),
            pltpu.VMEM((NZ, rows, hg), BF16),
            pltpu.VMEM((NZ, ts, hg), F32),
            pltpu.VMEM((NZ, ts, hg), F32),
            pltpu.VMEM((n_dp, NZ, piece, hg), BF16),
            pltpu.VMEM((n_dp, NZ, piece, hg), BF16),
            pltpu.VMEM((NZ, piece, hg), F32),
            pltpu.VMEM((NZ, piece, hg), F32),
            pltpu.VMEM((n_seq, 8, 256), F32),
            pltpu.VMEM((n_seq - 1, 8, 256), F32),
            *[dma(shape) for shape in sems],
        ],
        compiler_params=pltpu.CompilerParams(
            collective_id=0, has_side_effects=True, vmem_limit_bytes=58 * 1024 * 1024
        ),
        name="joint",
    )(
        caption_states[0],
        caption_gain[None],
        text_proj,
        slot_source,
        caption_len[None],
        query_gain[None],
        key_gain[None],
        image_q[0],
        image_k[0],
        image_v[0],
        out_weight,
        gate,
        d_out[0],
    )
    image_out, text_attn, d_attn, grad_wo, grad_gate = pl.pallas_call(
        copy_out,
        out_shape=out_shape,
        in_specs=[vmem] * 5,
        out_specs=(hbm,) * 5,
        scratch_shapes=[dma((5,))],
        name="copy_out",
    )(*outs)
    return (image_out[None], text_attn[None], d_attn[None], grad_wo, grad_gate)


def solution(mesh):
    in_specs = (
        P("dp", None, "seq"),
        P("seq"),
        P("seq", None),
        P("dp"),
        P("dp", None),
        P(),
        P(),
        P("dp", "seq", None),
        P("dp", "seq", None),
        P("dp", "seq", None),
        P(),
        P("dp", None),
        P("dp", "seq", None),
    )
    out_specs = (
        P("dp", "seq", None),
        P("dp", "seq", None),
        P("dp", "seq", None),
        P(("dp", "seq"), None),
        P("dp", "seq"),
    )
    return jax.shard_map(
        functools.partial(on_device, mesh.shape["dp"]),
        mesh=mesh,
        in_specs=in_specs,
        out_specs=out_specs,
        check_vma=False,
    )
```

time: 113 us -> 84.9 us (0.75)
  Pallas kernels: 99.7 us -> 83.4 us
  local copies, waits for them, and re-layouts: 9.91 us -> 0 us
  other arithmetic: 1.32 us -> 0 us
    pallas_call x1 -> x2, Pallas kernels: 99.7 us -> 83.4 us  [the longest x1 81 us: on_device(): pl.pallas_call(functools.partial(joint_kernel, n_dp), out_shape=out_shape...]
    unnamed x6 -> x0, local copies, waits for them, and re-layouts: 8.49 us -> none
    another operation x3 -> x0, local copies, waits for them, and re-layouts: 1.42 us -> none  [the longest x1 0.72 us: on_device(): sources[:, None]]
    unnamed x1 -> x0, other arithmetic: 1.32 us -> none
where the time goes in v2:
time: 84.9 us; the launch traced here: 84.7 us
  Pallas kernels  83.4 us (98%)
  between operations  1.29 us (2%)
    pallas_call x1, Pallas kernels, on_device(): pl.pallas_call(functools.partial(joint_kernel, n_dp), out_shape=out_shape...  81 us
    pallas_call x1, Pallas kernels, on_device(): pl.pallas_call(copy_out, out_shape=out_shape, in_specs=[vmem] * 5, out_sp...  2.43 us

profile of v2, /device:TPU:1, one launch (start us, length us, event | category | flops | bytes accessed | tf_op | source)
XLA Modules:
  0.0 84.7 jit_solution(2565696131533712327)
XLA Ops:
  1.3 81.0 %joint.1 = (bf16[128,3072]{1,0:T(8,128)(2,1)}, bf16[8,1536]{1,0:T(8,128)(2,1)}, bf16[128,1536]{1,0:T(8,128)(2,1)}, f32[24,1536]{1,0:T(8,128)}, f32[1,192]{1,0:T(1,128)}) custom-call(bf16[128,256]{1,0:T(8,128)(2,1)} %bitcast.17, f32[1,256]{1,0:T(1,128)} %bitcast.18, bf16[256,4608]{1,0:T(8,128)(2,1)} %text_proj_hbm.1, s32[1,128]{1,0:T(1,128)} %source_ref.1, ...), custom_call_target="tpu_custom_call" | custom-call | tf_op jit(solution)/shard_map/joint/pallas_call | solution.py:678
  82.3 2.4 %copy_out.1 = (bf16[128,3072]{1,0:T(8,128)(2,1)}, bf16[8,1536]{1,0:T(8,128)(2,1)}, bf16[128,1536]{1,0:T(8,128)(2,1)}, f32[24,1536]{1,0:T(8,128)}, f32[1,192]{1,0:T(1,128)}) custom-call(bf16[128,3072]{1,0:T(8,128)(2,1)} %get-tuple-element.15.refs_0_, bf16[8,1536]{1,0:T(8,128)(2,1)} %get-tuple-element.16.refs_1_, bf16[128,1536]{1,0:T(8,128)(2,1)} %get-tuple-element.17.refs_2_, ...), custom_call_target="tpu_custom_call" | custom-call | tf_op jit(solution)/shard_map/copy_out/pallas_call | solution.py:735

commit v3 on v2

--- a/solution.py
+++ b/solution.py
@@ -74,6 +74,9 @@
     fin,
     gsend,
     grecv,
+    image_buf,
+    d_attn_buf,
+    store_sem,
     load_sem,
     loc_sem,
     kvq_s,
@@ -144,27 +147,11 @@
             device_id_type=pl.DeviceIdType.MESH,
         )
 
-    load_tp = pltpu.make_async_copy(text_proj_hbm, tp, load_sem.at[0])
-    load_dout = pltpu.make_async_copy(dout_hbm, dout, load_sem.at[1])
-    load_wo = pltpu.make_async_copy(wo_hbm, wo, load_sem.at[2])
-    load_tp.start()
-    load_dout.start()
-    load_wo.start()
-
     def col(index):
         return pl.ds(pl.multiple_of(index * hg, 128), hg)
 
     def kv_rows(q_from, z_from):
         return pl.ds(pl.multiple_of((q_from * NZ + z_from) * rows, 128), rows)
-
-    own_rows = kv_rows(q, z)
-    own = [
-        pltpu.make_async_copy(k_hbm.at[:, col(z)], kv.at[0, own_rows, :], loc_sem.at[0]),
-        pltpu.make_async_copy(v_hbm.at[:, col(z)], kv.at[1, own_rows, :], loc_sem.at[1]),
-        pltpu.make_async_copy(q_hbm.at[:, col(z)], qi.at[z], loc_sem.at[2]),
-    ]
-    for copy in own:
-        copy.start()
 
     barrier = pltpu.get_barrier_semaphore()
 
@@ -186,6 +173,22 @@
                 device_id={"dp": (dp + offset) % n_dp, "seq": at_z(z_to)},
                 device_id_type=pl.DeviceIdType.MESH,
             )
+
+    own_rows = kv_rows(q, z)
+    own = [
+        pltpu.make_async_copy(k_hbm.at[:, col(z)], kv.at[0, own_rows, :], loc_sem.at[0]),
+        pltpu.make_async_copy(v_hbm.at[:, col(z)], kv.at[1, own_rows, :], loc_sem.at[1]),
+        pltpu.make_async_copy(q_hbm.at[:, col(z)], qi.at[z], loc_sem.at[2]),
+    ]
+    for copy in own:
+        copy.start()
+
+    load_tp = pltpu.make_async_copy(text_proj_hbm, tp, load_sem.at[0])
+    load_dout = pltpu.make_async_copy(dout_hbm, dout, load_sem.at[1])
+    load_wo = pltpu.make_async_copy(wo_hbm, wo, load_sem.at[2])
+    load_tp.start()
+    load_dout.start()
+    load_wo.start()
 
     pl.semaphore_wait(barrier, n_seq - 1 + NZ * (n_dp - 1))
 
@@ -315,13 +318,18 @@
     load_wo.wait()
     for t in range(inner // 256):
         cols = slice(t * 256, (t + 1) * 256)
-        d_attn_ref[:, cols] = jnp.dot(g[...], wo[:, cols], preferred_element_type=F32).astype(BF16)
+        d_attn_buf[:, cols] = jnp.dot(g[...], wo[:, cols], preferred_element_type=F32).astype(BF16)
+    store_d_attn = pltpu.make_async_copy(d_attn_buf, d_attn_ref, store_sem.at[0])
+    store_d_attn.start()
 
     for dz in (1, 3, 2):
         kvq[dz][0].wait_recv()
         kvq[dz][1].wait_recv()
         for copy in forward(dz):
             copy.start()
+
+    g1[0].start()
+    g1[2].start()
 
     for copy in y_copies:
         copy.wait_recv()
@@ -378,9 +386,6 @@
         dz = (0, 1, 3, 2)[i]
         forward(dz)[0].wait_recv()
         relay(dz).start()
-        if i == 1:
-            g1[0].start()
-            g1[2].start()
 
     def add_square(offset, total):
         square_copy(offset).wait_recv()
@@ -519,10 +524,13 @@
     for t in range(n_seq // 2):
         cols = slice(t * 2 * per, (t + 1) * 2 * per)
         projected = lax.dot_general(image_attn, wo[cols, :], NT, preferred_element_type=F32)
-        image_out_ref[:, cols] = (gate_ref[:, cols] * projected).astype(BF16)
+        image_buf[:, cols] = (gate_ref[:, cols] * projected).astype(BF16)
         term = jnp.sum(projected * dout[:, cols].astype(F32), axis=0, keepdims=True)
         gsend[2 * t, :, :per] = jnp.broadcast_to(term[:, :per], (8, per))
         gsend[2 * t + 1, :, :per] = jnp.broadcast_to(term[:, per:], (8, per))
+
+    store_image = pltpu.make_async_copy(image_buf, image_out_ref, store_sem.at[1])
+    store_image.start()
 
     def gate_copy(offset):
         target = (me + offset) % n_seq
@@ -597,6 +605,8 @@
     for zz in range(NZ):
         grad_wo_ref[:, zz * hg : (zz + 1) * hg] = fin[zz]
 
+    store_d_attn.wait()
+    store_image.wait()
     for dz in range(1, NZ):
         for copy in kvq[dz]:
             copy.wait_send()
@@ -679,7 +689,7 @@
         functools.partial(joint_kernel, n_dp),
         out_shape=out_shape,
         in_specs=[vmem, vmem, hbm, vmem, vmem, vmem, vmem, hbm, hbm, hbm, hbm, vmem, hbm],
-        out_specs=(vmem,) * 5,
+        out_specs=(hbm, vmem, hbm, vmem, vmem),
         scratch_shapes=[
             pltpu.VMEM(text_proj.shape, BF16),
             pltpu.VMEM(out_weight.shape, BF16),
@@ -711,6 +721,9 @@
             pltpu.VMEM((NZ, piece, hg), F32),
             pltpu.VMEM((n_seq, 8, 256), F32),
             pltpu.VMEM((n_seq - 1, 8, 256), F32),
+            pltpu.VMEM((rows, d_model), BF16),
+            pltpu.VMEM((rows, inner), BF16),
+            dma((2,)),
             *[dma(shape) for shape in sems],
         ],
         compiler_params=pltpu.CompilerParams(

time: 84.9 us -> 84.4 us (level)
  no operation moved by 1% of the time
where the time goes in v3:
time: 84.4 us; the launch traced here: 84.2 us
  Pallas kernels  83 us (98%)
  between operations  1.29 us (2%)
    pallas_call x1, Pallas kernels, on_device(): pl.pallas_call(functools.partial(joint_kernel, n_dp), out_shape=out_shape...  80.5 us
    pallas_call x1, Pallas kernels, on_device(): pl.pallas_call(copy_out, out_shape=out_shape, in_specs=[vmem] * 5, out_sp...  2.43 us

profile of v3, /device:TPU:1, one launch (start us, length us, event | category | flops | bytes accessed | tf_op | source)
XLA Modules:
  0.0 84.2 jit_solution(8374114501860306201)
XLA Ops:
  1.3 80.5 %joint.1 = (bf16[128,3072]{1,0:T(8,128)(2,1)}, bf16[8,1536]{1,0:T(8,128)(2,1)}, bf16[128,1536]{1,0:T(8,128)(2,1)}, f32[24,1536]{1,0:T(8,128)}, f32[1,192]{1,0:T(1,128)}) custom-call(bf16[128,256]{1,0:T(8,128)(2,1)} %bitcast.17, f32[1,256]{1,0:T(1,128)} %bitcast.18, bf16[256,4608]{1,0:T(8,128)(2,1)} %text_proj_hbm.1, s32[1,128]{1,0:T(1,128)} %source_ref.1, ...), custom_call_target="tpu_custom_call" | custom-call | tf_op jit(solution)/shard_map/joint/pallas_call | solution.py:688
  81.8 2.4 %copy_out.1 = (bf16[128,3072]{1,0:T(8,128)(2,1)}, bf16[8,1536]{1,0:T(8,128)(2,1)}, bf16[128,1536]{1,0:T(8,128)(2,1)}, f32[24,1536]{1,0:T(8,128)}, f32[1,192]{1,0:T(1,128)}) custom-call(bf16[128,3072]{1,0:T(8,128)(2,1)} %get-tuple-element.15.refs_0_, bf16[8,1536]{1,0:T(8,128)(2,1)} %get-tuple-element.16.refs_1_, bf16[128,1536]{1,0:T(8,128)(2,1)} %get-tuple-element.17.refs_2_, ...), custom_call_target="tpu_custom_call" | custom-call | tf_op jit(solution)/shard_map/copy_out/pallas_call | solution.py:748

commit v4 on v3

--- a/solution.py
+++ b/solution.py
@@ -481,12 +481,13 @@
             result = attend(qi[z_to, :, cols], h, near)
             a_all[kv_rows(q, z_to), cols] = result.astype(BF16)
 
+        for copy in a_plane(i):
+            copy.start()
+
         @pl.when(i < NZ - 1)
         def _():
             a_return(i).start()
 
-        for copy in a_plane(i):
-            copy.start()
         k = (i % 2) * 2 + i // 2
         source = g_source(k)
         g_ahead(k, source)[0].wait_recv()

time: 84.4 us -> 84.4 us (level)
  no operation moved by 1% of the time
where the time goes in v4:
time: 84.4 us; the launch traced here: 84.2 us
  Pallas kernels  83 us (98%)
  between operations  1.29 us (2%)
    pallas_call x1, Pallas kernels, on_device(): pl.pallas_call(functools.partial(joint_kernel, n_dp), out_shape=out_shape...  80.5 us
    pallas_call x1, Pallas kernels, on_device(): pl.pallas_call(copy_out, out_shape=out_shape, in_specs=[vmem] * 5, out_sp...  2.43 us

profile of v4, /device:TPU:1, one launch (start us, length us, event | category | flops | bytes accessed | tf_op | source)
XLA Modules:
  0.0 84.2 jit_solution(15877860751327221395)
XLA Ops:
  1.3 80.5 %joint.1 = (bf16[128,3072]{1,0:T(8,128)(2,1)}, bf16[8,1536]{1,0:T(8,128)(2,1)}, bf16[128,1536]{1,0:T(8,128)(2,1)}, f32[24,1536]{1,0:T(8,128)}, f32[1,192]{1,0:T(1,128)}) custom-call(bf16[128,256]{1,0:T(8,128)(2,1)} %bitcast.17, f32[1,256]{1,0:T(1,128)} %bitcast.18, bf16[256,4608]{1,0:T(8,128)(2,1)} %text_proj_hbm.1, s32[1,128]{1,0:T(1,128)} %source_ref.1, ...), custom_call_target="tpu_custom_call" | custom-call | tf_op jit(solution)/shard_map/joint/pallas_call | solution.py:689
  81.8 2.4 %copy_out.1 = (bf16[128,3072]{1,0:T(8,128)(2,1)}, bf16[8,1536]{1,0:T(8,128)(2,1)}, bf16[128,1536]{1,0:T(8,128)(2,1)}, f32[24,1536]{1,0:T(8,128)}, f32[1,192]{1,0:T(1,128)}) custom-call(bf16[128,3072]{1,0:T(8,128)(2,1)} %get-tuple-element.15.refs_0_, bf16[8,1536]{1,0:T(8,128)(2,1)} %get-tuple-element.16.refs_1_, bf16[128,1536]{1,0:T(8,128)(2,1)} %get-tuple-element.17.refs_2_, ...), custom_call_target="tpu_custom_call" | custom-call | tf_op jit(solution)/shard_map/copy_out/pallas_call | solution.py:749
